TPU v7x, 32 devices: a whole 2x2x4 slice. The times are simulated.
32 devices in a mesh: dp: 16 (over z, x, core), seq: 2 (over y).
Axes of the slice: x: 2, y: 2, z: 4, core: 2. Of those that a mesh axis runs over, the one named last changes fastest.
Arguments:
- hidden_in: bfloat16 [32, 1024, 1024], P('dp', 'seq'), may hold values from -6 to 6
- family: int32 [16], P('dp'), may hold values from 0 to 63
- orient: int32 [32], P('dp'), may hold values from 0 to 1, as said below
- norm_gain: bfloat16 [1024], replicated, may hold values from 0.099609375 to 1.8984375
- norm_bias: bfloat16 [1024], replicated, may hold values from -4 to 4
- qkv_weight: bfloat16 [1024, 3072], replicated, may hold values from -0.1875 to 0.1875
- out_weight: bfloat16 [1024, 1024], replicated, may hold values from -0.5 to 0.5
- up_weight: bfloat16 [1024, 4096], replicated, may hold values from -0.1875 to 0.1875
- up_bias: bfloat16 [4096], replicated, may hold values from -6 to 6
- down_weight: bfloat16 [4096, 1024], replicated, may hold values from -0.09375 to 0.09375
- down_bias: bfloat16 [1024], replicated, may hold values from -4 to 4
- family_table: bfloat16 [64, 1024], replicated, may hold values from -6 to 6
- orient_table: bfloat16 [2, 1024], replicated, may hold values from -6 to 6
- cotangent: bfloat16 [32, 1024, 1024], P('dp', 'seq'), may hold values from -6 to 6
Outputs:
- layer_out: bfloat16 [32, 1024, 1024], P('dp', 'seq')
- input_grad: float32 [32, 1024, 1024], P('dp', 'seq')
- norm_gain_grad: float32 [1024], replicated
- norm_bias_grad: float32 [1024], replicated
- qkv_weight_grad: float32 [1024, 3072], P(('dp', 'seq'))
- out_weight_grad: float32 [1024, 1024], P(('dp', 'seq'))
- up_weight_grad: float32 [1024, 4096], P(('dp', 'seq'))
- up_bias_grad: float32 [4096], replicated
- down_weight_grad: float32 [4096, 1024], P(('dp', 'seq'))
- down_bias_grad: float32 [1024], replicated
- family_table_grad: float32 [64, 1024], replicated
- orient_table_grad: float32 [2, 1024], replicated
Inputs may be any that keep to these rules, and one draw needn't show every extreme that they name: `orient`: in each pair of rows 2p and 2p + 1 one row has flag 0 and the other flag 1.
All inputs are finite; a program needn't handle non-finite values.
Results may differ from a plain program's by a relative error of at most 0.006.
Values may be sent and summed in bfloat16 or wider, within the bound.
A program may use at most 256 MiB of HBM per device.

v0:
```python
import math
import jax
import jax.numpy as jnp
from jax import lax
from jax.sharding import PartitionSpec as P

H = 16
HD = 64
ROT = 32


def for_sending(shard):

    def short(part):
        return part.astype(jnp.bfloat16) if part.dtype == jnp.float32 else part

    return jax.tree.map(short, shard)


def rope_tables(positions, features):
    column = jnp.arange(features, dtype=jnp.int32)
    within = column % HD
    frequency = jnp.exp(-(2.0 * (within // 2).astype(jnp.float32) / ROT) * math.log(10000.0))
    angles = positions[:, None] * frequency[None, :]
    rotary = within < ROT
    cosine = jnp.where(rotary[None, :], jnp.cos(angles), 1.0)
    sign_term = jnp.where(within % 2 == 0, -1.0, 1.0)
    sine_term = jnp.where(rotary[None, :], sign_term[None, :] * jnp.sin(angles), 0.0)
    return (cosine, sine_term)


def pair_swap(values):
    even_cols = jnp.arange(values.shape[-1]) % 2 == 0
    return jnp.where(even_cols, jnp.roll(values, -1, axis=-1), jnp.roll(values, 1, axis=-1))


def rotate(values, cosine, sine_term):
    return values * cosine + pair_swap(values) * sine_term


def rotate_back(values, cosine, sine_term):
    return values * cosine + pair_swap(values * sine_term)


def gelu_tanh(pre_values):
    return jax.nn.gelu(pre_values, approximate=True)


def body(
    hidden_in,
    family,
    orient,
    norm_gain,
    norm_bias,
    qkv_weight,
    out_weight,
    up_weight,
    up_bias,
    down_weight,
    down_bias,
    family_table,
    orient_table,
    cotangent,
):
    seq_count = lax.axis_size("seq")
    row_count, seg_length, features = hidden_in.shape
    full_length = seg_length * seq_count
    local_heads = H // seq_count
    head_size = features // H
    slab_width = features // seq_count
    block_rows = min(512, full_length)
    block_count = full_length // block_rows
    score_scale = head_size ** (-0.5)
    token_count = row_count * seg_length
    family_rows = jnp.repeat(family, 2)
    family_hot = (family_rows[:, None] == jnp.arange(family_table.shape[0])[None, :]).astype(
        jnp.bfloat16
    )
    orient_hot = (orient[:, None] == jnp.arange(2)[None, :]).astype(jnp.bfloat16)
    embedding = jnp.dot(family_hot, family_table, preferred_element_type=jnp.float32) + jnp.dot(
        orient_hot, orient_table, preferred_element_type=jnp.float32
    )
    embedded = (hidden_in.astype(jnp.float32) + embedding[:, None, :]).reshape(
        token_count, features
    )
    row_mean = jnp.mean(embedded, -1, keepdims=True)
    centred = embedded - row_mean
    row_var = jnp.mean(centred * centred, -1, keepdims=True)
    inv_std = lax.rsqrt(row_var + 1e-05)
    normed_hat = centred * inv_std
    gain_f32 = norm_gain.astype(jnp.float32)
    normed_low = (normed_hat * gain_f32 + norm_bias.astype(jnp.float32)).astype(jnp.bfloat16)
    projected = jnp.dot(normed_low, qkv_weight, preferred_element_type=jnp.float32).reshape(
        row_count, seg_length, 3 * features
    )
    positions = (lax.axis_index("seq") * seg_length + jnp.arange(seg_length)).astype(jnp.float32)
    cosine, sine_term = rope_tables(positions, features)
    queries = rotate(projected[..., :features], cosine, sine_term).astype(jnp.bfloat16)
    keys_rot = rotate(projected[..., features : 2 * features], cosine, sine_term).astype(
        jnp.bfloat16
    )
    values = projected[..., 2 * features :].astype(jnp.bfloat16)
    query_heads, key_heads, value_heads = (
        lax.all_to_all(queries, "seq", split_axis=2, concat_axis=1, tiled=True),
        lax.all_to_all(keys_rot, "seq", split_axis=2, concat_axis=1, tiled=True),
        lax.all_to_all(values, "seq", split_axis=2, concat_axis=1, tiled=True),
    )

    def scores_for(query_block, key_rows, block_start):
        logits = (
            jnp.einsum("qhd,khd->hqk", query_block, key_rows, preferred_element_type=jnp.float32)
            * score_scale
        )
        causal = (block_start + jnp.arange(block_rows))[:, None] >= jnp.arange(full_length)[None, :]
        return jnp.where(causal[None], logits, -1e30)

    def attend(row_args):
        query_row, key_row, value_row = row_args
        key_rows = key_row.reshape(full_length, local_heads, head_size)
        value_rows = value_row.reshape(full_length, local_heads, head_size)
        pieces = []
        log_parts = []
        for block_index in range(block_count):
            block_start = block_index * block_rows
            query_block = query_row[block_start : block_start + block_rows].reshape(
                block_rows, local_heads, head_size
            )
            logits = scores_for(query_block, key_rows, block_start)
            row_peak = jnp.max(logits, -1, keepdims=True)
            weights = jnp.exp(logits - row_peak)
            row_total = jnp.sum(weights, -1, keepdims=True)
            prob_low = (weights / row_total).astype(jnp.bfloat16)
            output_block = jnp.einsum(
                "hqk,khd->qhd", prob_low, value_rows, preferred_element_type=jnp.float32
            )
            pieces.append(output_block.reshape(block_rows, slab_width).astype(jnp.bfloat16))
            log_parts.append((row_peak + jnp.log(row_total))[..., 0])
        return (jnp.concatenate(pieces, 0), jnp.concatenate(log_parts, 1))

    attended_heads, log_sums = lax.map(attend, (query_heads, key_heads, value_heads))
    attended = jax.tree.map(
        lambda part, own: part.astype(own.dtype),
        lax.all_to_all(for_sending(attended_heads), "seq", split_axis=1, concat_axis=2, tiled=True),
        attended_heads,
    )
    attended_flat = attended.reshape(token_count, features)
    branch_attn = jnp.dot(attended_flat, out_weight, preferred_element_type=jnp.float32)
    up_pre = jnp.dot(normed_low, up_weight, preferred_element_type=jnp.float32) + up_bias.astype(
        jnp.float32
    )
    up_act = gelu_tanh(up_pre).astype(jnp.bfloat16)
    branch_feed = jnp.dot(
        up_act, down_weight, preferred_element_type=jnp.float32
    ) + down_bias.astype(jnp.float32)
    layer_out = (
        (embedded + branch_attn + branch_feed)
        .astype(jnp.bfloat16)
        .reshape(row_count, seg_length, features)
    )
    grad_low = cotangent.reshape(token_count, features)
    grad_f32 = grad_low.astype(jnp.float32)
    down_grad = jnp.einsum("nf,nd->fd", up_act, grad_low, preferred_element_type=jnp.float32)
    down_bias_grad = jnp.sum(grad_f32, 0)
    act_grad = jnp.einsum("nd,fd->nf", grad_low, down_weight, preferred_element_type=jnp.float32)
    gelu_out, gelu_pull = jax.vjp(gelu_tanh, up_pre)
    pre_grad = gelu_pull(act_grad)[0].astype(jnp.bfloat16)
    up_bias_grad = jnp.sum(pre_grad.astype(jnp.float32), 0)
    up_grad = jnp.einsum("nd,nf->df", normed_low, pre_grad, preferred_element_type=jnp.float32)
    normed_grad = jnp.einsum("nf,df->nd", pre_grad, up_weight, preferred_element_type=jnp.float32)
    out_grad = jnp.einsum("nd,ne->de", attended_flat, grad_low, preferred_element_type=jnp.float32)
    attended_grad = jnp.einsum(
        "ne,de->nd", grad_low, out_weight, preferred_element_type=jnp.float32
    )
    attended_grad = attended_grad.astype(jnp.bfloat16).reshape(row_count, seg_length, features)
    grad_heads = lax.all_to_all(attended_grad, "seq", split_axis=2, concat_axis=1, tiled=True)

    def attend_back(row_args):
        query_row, key_row, value_row, grad_row, log_row = row_args
        key_rows = key_row.reshape(full_length, local_heads, head_size)
        value_rows = value_row.reshape(full_length, local_heads, head_size)
        keys_total = jnp.zeros((full_length, local_heads, head_size), jnp.float32)
        values_total = jnp.zeros((full_length, local_heads, head_size), jnp.float32)
        query_parts = []
        for block_index in range(block_count):
            block_start = block_index * block_rows
            query_block = query_row[block_start : block_start + block_rows].reshape(
                block_rows, local_heads, head_size
            )
            grad_block = grad_row[block_start : block_start + block_rows].reshape(
                block_rows, local_heads, head_size
            )
            logits = scores_for(query_block, key_rows, block_start)
            probs_full = jnp.exp(logits - log_row[:, block_start : block_start + block_rows, None])
            prob_low = probs_full.astype(jnp.bfloat16)
            probs_grad = jnp.einsum(
                "qhd,khd->hqk", grad_block, value_rows, preferred_element_type=jnp.float32
            )
            inner_sum = jnp.sum(probs_full * probs_grad, -1, keepdims=True)
            scores_grad = (probs_full * (probs_grad - inner_sum)).astype(jnp.bfloat16)
            values_total = values_total + jnp.einsum(
                "hqk,qhd->khd", prob_low, grad_block, preferred_element_type=jnp.float32
            )
            query_grad = (
                jnp.einsum(
                    "hqk,khd->qhd", scores_grad, key_rows, preferred_element_type=jnp.float32
                )
                * score_scale
            )
            query_parts.append(query_grad.reshape(block_rows, slab_width).astype(jnp.bfloat16))
            keys_total = (
                keys_total
                + jnp.einsum(
                    "hqk,qhd->khd", scores_grad, query_block, preferred_element_type=jnp.float32
                )
                * score_scale
            )
        return (
            jnp.concatenate(query_parts, 0),
            keys_total.reshape(full_length, slab_width).astype(jnp.bfloat16),
            values_total.reshape(full_length, slab_width).astype(jnp.bfloat16),
        )

    query_grad_heads, key_grad_heads, value_grad_heads = lax.map(
        attend_back, (query_heads, key_heads, value_heads, grad_heads, log_sums)
    )
    query_grad_pos, key_grad_pos, value_grad_pos = (
        lax.all_to_all(
            for_sending(query_grad_heads), "seq", split_axis=1, concat_axis=2, tiled=True
        ).astype(query_grad_heads.dtype),
        lax.all_to_all(
            for_sending(key_grad_heads), "seq", split_axis=1, concat_axis=2, tiled=True
        ).astype(key_grad_heads.dtype),
        lax.all_to_all(
            for_sending(value_grad_heads), "seq", split_axis=1, concat_axis=2, tiled=True
        ).astype(value_grad_heads.dtype),
    )
    projected_grad = jnp.concatenate(
        [
            rotate_back(query_grad_pos.astype(jnp.float32), cosine, sine_term),
            rotate_back(key_grad_pos.astype(jnp.float32), cosine, sine_term),
            value_grad_pos.astype(jnp.float32),
        ],
        -1,
    )
    projected_grad = projected_grad.astype(jnp.bfloat16).reshape(token_count, 3 * features)
    qkv_grad = jnp.einsum(
        "nd,ne->de", normed_low, projected_grad, preferred_element_type=jnp.float32
    )
    normed_grad = normed_grad + jnp.einsum(
        "ne,de->nd", projected_grad, qkv_weight, preferred_element_type=jnp.float32
    )
    gain_grad = jnp.sum(normed_grad * normed_hat, 0)
    bias_grad = jnp.sum(normed_grad, 0)
    scaled_grad = normed_grad * gain_f32
    hat_grad = (
        scaled_grad
        - jnp.mean(scaled_grad, -1, keepdims=True)
        - normed_hat * jnp.mean(scaled_grad * normed_hat, -1, keepdims=True)
    )
    input_grad = (grad_f32 + inv_std * hat_grad).reshape(row_count, seg_length, features)
    row_sums = jnp.sum(input_grad, 1)
    family_grad = jnp.einsum(
        "rf,rd->fd", family_hot.astype(jnp.float32), row_sums, precision=lax.Precision.HIGHEST
    )
    orient_grad = jnp.einsum(
        "rf,rd->fd", orient_hot.astype(jnp.float32), row_sums, precision=lax.Precision.HIGHEST
    )
    gain_sum, bias_sum, up_bias_sum, down_bias_sum, family_sum, orient_sum = lax.psum(
        (gain_grad, bias_grad, up_bias_grad, down_bias_grad, family_grad, orient_grad),
        ("dp", "seq"),
    )
    qkv_sum, out_sum, up_sum, down_sum = (
        lax.psum_scatter(qkv_grad, ("dp", "seq"), scatter_dimension=0, tiled=True),
        lax.psum_scatter(out_grad, ("dp", "seq"), scatter_dimension=0, tiled=True),
        lax.psum_scatter(up_grad, ("dp", "seq"), scatter_dimension=0, tiled=True),
        lax.psum_scatter(down_grad, ("dp", "seq"), scatter_dimension=0, tiled=True),
    )
    return (
        layer_out,
        input_grad,
        gain_sum,
        bias_sum,
        qkv_sum,
        out_sum,
        up_sum,
        up_bias_sum,
        down_sum,
        down_bias_sum,
        family_sum,
        orient_sum,
    )


def solution(mesh):
    return jax.shard_map(
        body,
        mesh=mesh,
        in_specs=(
            P("dp", "seq", None),
            P("dp"),
            P("dp"),
            P(),
            P(),
            P(),
            P(),
            P(),
            P(),
            P(),
            P(),
            P(),
            P(),
            P("dp", "seq", None),
        ),
        out_specs=(
            P("dp", "seq", None),
            P("dp", "seq", None),
            P(),
            P(),
            P(("dp", "seq"), None),
            P(("dp", "seq"), None),
            P(("dp", "seq"), None),
            P(),
            P(("dp", "seq"), None),
            P(),
            P(),
            P(),
        ),
        check_vma=False,
    )
```

profile of v0, /device:TPU:0, one launch (start us, length us, event | category | flops | bytes accessed | tf_op | source)
XLA Modules:
  0.0 1835.5 jit_solution(17062700725585724504)
XLA Ops:
  15.1 7.0 fusion.30
  22.1 8.0 fusion.89
  33.1 7.5 fusion.48
  40.6 12.5 fusion.37
  53.2 6.2 copy.51
  64.3 6.2 copy.53
  70.5 20.2 %all-to-all-done.1 = bf16[2,512,1024]{1,0,2:T(2,128)(2,1)} async-done(((bf16[2,512,1024]{1,0,2:T(2,128)(2,1)}), bf16[2,512,1024]{1,0,2:T(2,128)(2,1)}, u32[]{:S(2)}, u32[]{:S(2)}) %all-to-all-start.1) | async-done | bytes 2097184 | tf_op jit(solution)/shard_map/all_to_all | solution.py:104
  99.4 6.2 copy.49
  105.6 14.7 all-to-all-done.2
  125.1 5.3 convolution_convert_fusion
  130.4 6.2 copy.57
  176.7 84.7 %while.26 = (s32[]{:T(128)}, bf16[2,1024,512]{1,2,0:T(8,128)(2,1)}, f32[2,8,1024]{2,1,0:T(8,128)S(1)}, bf16[2,1024,512]{1,2,0:T(8,128)(2,1)}, bf16[2,1024,512]{1...) while((s32[]{:T(128)}, bf16[2,1024,512]{1,2,0:T(8,128)(2,1)}, ...), condition=%wide.region_7.8_spmd, body=%wide.region_2.7_spmd.sunk | while | flops 2251817472 | bytes 124064400 | solution.py:140
  188.6 7.4 fusion.195
  196.1 8.1 fusion.196
  204.2 5.6 fusion.200
  209.8 8.2 fusion.197
  231.0 7.4 fusion.195
  238.4 8.1 fusion.196
  246.6 5.6 fusion.200
  252.1 8.2 fusion.197
  275.8 202.6 %while.27 = (s32[]{:T(128)}, bf16[2,1024,512]{1,2,0:T(8,128)(2,1)}, bf16[2,1024,512]{1,2,0:T(8,128)(2,1)}, bf16[2,1024,512]{1,2,0:T(8,128)(2,1)}, bf16[2,1024,51...) while((s32[]{:T(128)}, bf16[2,1024,512]{1,2,0:T(8,128)(2,1)}, ...), condition=%wide.region_11.12_spmd, body=%wide.region_8.11_spmd.sunk | while | flops 5451014656 | bytes 458462208 | solution.py:223
  278.6 8.1 fusion.226
  287.1 12.6 multiply_reduce_fusion.9
  299.8 11.3 multiply_convert_fusion.10
  314.4 8.1 fusion.223
  322.9 12.6 multiply_reduce_fusion.8
  335.5 11.3 multiply_convert_fusion.9
  352.2 6.6 fusion.227
  358.8 7.5 fusion.228
  367.9 6.2 fusion.225
  379.6 8.1 fusion.226
  388.2 12.6 multiply_reduce_fusion.9
  400.8 11.3 multiply_convert_fusion.10
  415.4 8.1 fusion.223
  423.9 12.6 multiply_reduce_fusion.8
  436.5 11.3 multiply_convert_fusion.9
  453.2 6.5 fusion.227
  459.8 7.5 fusion.228
  468.9 6.2 fusion.225
  478.4 6.2 copy.59
  489.4 16.0 fusion.98
  505.4 6.2 copy.63
  517.9 26.5 %convert_reduce_fusion = (f32[4096]{0:T(1024)}, bf16[1024,4096]{1,0:T(8,128)(2,1)}) fusion(f32[1024,4096]{1,0:T(8,128)} %fusion.98, f32[4096]{0:T(1024)S(1)} %copy-done.35, bf16[1024,1024]{1,0:T(8,128)(2,1)} %bitcast.316, bf16[4096,1024]{1,0:T(8,128)(2,1)} %param.27), kind=kOutput, calls=%fused_computation.70 | convolution fusion | flops 8686399488 | bytes 35684352 | tf_op jit(solution)/shard_map/nd,fd->nf/dot_general | solution.py:164
  544.4 6.2 copy.67
  550.6 6.3 copy.55
  556.9 5.8 copy.78
  562.7 5.8 copy.60
  573.3 5.8 copy.77
  579.1 5.7 copy.64
  584.8 6.8 reshape.472
  591.6 6.7 reshape.474
  598.3 5.4 broadcast_multiply_fusion.1
  632.7 9.5 fusion.33
  642.3 13.1 fusion.46
  655.5 15.7 multiply_reduce_fusion.2
  687.5 12.8 fusion.45
  700.6 16.2 fusion.100
  716.9 20.2 %fusion.85 = f32[4096,1024]{1,0:T(8,128)} fusion(bf16[1024,1024]{1,0:T(8,128)(2,1)} %bitcast.317, f32[1024,4096]{1,0:T(8,128)} %fusion.98, f32[4096]{0:T(1024)S(1)} %copy-done.35), kind=kOutput, calls=%fused_computation.174 | convolution fusion | flops 8631877632 | bytes 35667968 | tf_op jit(solution)/shard_map/nf,nd->fd/dot_general | solution.py:162
  740.0 42.0 %all-reduce = (f32[1024]{0:T(1024)}, f32[1024]{0:T(1024)}, f32[4096]{0:T(1024)}, f32[1024]{0:T(1024)}, f32[2,1024]{1,0:T(2,128)}) all-reduce(f32[1024]{0:T(1024)S(1)} %get-tuple-element.99, f32[1024]{0:T(1024)S(1)} %get-tuple-element.102, f32[4096]{0:T(1024)S(1)} %copy-done.36, ...), channel_id=1, replica_groups=mesh['dp'=16,'seq'=2] {'dp','seq'}, use_global_device_ids=true, to_apply=%region_15.16 | all-reduce | flops 9216 | bytes 73728 | tf_op jit(solution)/shard_map/psum | solution.py:268
  786.1 17.8 fusion.43
  803.9 143.2 %reduce-scatter.7.cloned.1.call-done = f32[32,1024]{1,0:T(8,128)} async-done(((f32[1024,1024]{1,0:T(8,128)}), f32[32,1024]{1,0:T(8,128)}) %reduce-scatter.7.cloned.1.call-update) | async-done | bytes 131088 | tf_op jit(solution)/shard_map/reduce_scatter | solution.py:274
  947.1 159.3 %reduce-scatter.5.cloned.1.call-done = f32[32,3072]{1,0:T(8,128)} async-done(((f32[1024,3072]{1,0:T(8,128)}), f32[32,3072]{1,0:T(8,128)}) %reduce-scatter.5.cloned.1.call-update) | async-done | bytes 393232 | tf_op jit(solution)/shard_map/reduce_scatter | solution.py:273
  1106.4 359.3 %reduce-scatter.9.cloned.1.call-done = f32[32,4096]{1,0:T(8,128)} async-done(((f32[1024,4096]{1,0:T(8,128)}), f32[32,4096]{1,0:T(8,128)}) %reduce-scatter.9.cloned.1.call-update) | async-done | bytes 524304 | tf_op jit(solution)/shard_map/reduce_scatter | solution.py:275
  1465.6 361.3 %reduce-scatter.11.cloned.1.call-done = f32[128,1024]{1,0:T(8,128)} async-done(((f32[4096,1024]{1,0:T(8,128)}), f32[128,1024]{1,0:T(8,128)}) %reduce-scatter.11.cloned.1.call-update) | async-done | bytes 524304 | tf_op jit(solution)/shard_map/reduce_scatter | solution.py:276
  (258 shorter events, 212.0 us)
Async XLA Ops:
  7.2 117.9 %copy-start = (bf16[1024,1024]{1,0:T(8,128)(2,1)S(1)}, bf16[1024,1024]{1,0:T(8,128)(2,1)}, u32[]{:S(2)}) copy-start(bf16[1024,1024]{1,0:T(8,128)(2,1)} %param.24) | copy-start | bytes 6291460
  7.2 7.0 copy-start.19
  10.1 5.0 copy-start.42
  10.1 5.0 copy-start.43
  10.1 5.0 copy-start.45
  15.1 122.1 %copy-start.29 = (f32[1024]{0:T(1024)}, f32[1024]{0:T(1024)S(1)}, u32[]{:S(2)}) copy-start(f32[1024]{0:T(1024)S(1)} %convert_element_type.207) | copy-start | bytes 12292
  22.0 9.6 copy-start.5
  33.0 20.2 %copy-start.38 = (pred[1024]{0:T(1024)(128)(4,1)}, pred[1024]{0:T(1024)(128)(4,1)S(1)}, u32[]{:S(2)}) copy-start(pred[1024]{0:T(1024)(128)(4,1)S(1)} %fusion.61) | copy-start | bytes 3076
  33.0 7.6 copy-start.16
  40.6 12.6 copy-start.9
  40.6 12.6 copy-start.11
  59.3 31.4 %all-to-all-start.1 = ((bf16[2,512,1024]{1,0,2:T(2,128)(2,1)}), bf16[2,512,1024]{1,0,2:T(2,128)(2,1)}, u32[]{:S(2)}, u32[]{:S(2)}) async-start(bf16[2,512,1024]{1,0,2:T(2,128)(2,1)} %copy.51), calls=%async_computation.1 | async-start | bytes 4194304 | tf_op jit(solution)/shard_map/all_to_all | solution.py:104
  90.8 29.5 %all-to-all-start.2 = ((bf16[2,512,1024]{1,0,2:T(2,128)(2,1)}), bf16[2,512,1024]{1,0,2:T(2,128)(2,1)}, u32[]{:S(2)}, u32[]{:S(2)}) async-start(bf16[2,512,1024]{1,0,2:T(2,128)(2,1)} %copy.53), calls=%async_computation.2 | async-start | bytes 4194304 | tf_op jit(solution)/shard_map/all_to_all | solution.py:105
  120.2 40.2 %all-to-all-start = ((bf16[2,512,1024]{1,0,2:T(2,128)(2,1)}), bf16[2,512,1024]{1,0,2:T(2,128)(2,1)}, u32[]{:S(2)}, u32[]{:S(2)}) async-start(bf16[2,512,1024]{1,0,2:T(2,128)(2,1)} %copy.49), calls=%async_computation | async-start | bytes 4194304 | tf_op jit(solution)/shard_map/all_to_all | solution.py:106
  130.4 6.2 copy-start.37
  136.5 4.9 copy-start.31
  136.5 4.9 copy-start.33
  160.4 101.0 %all-to-all-start.4 = ((bf16[2,512,1024]{1,0,2:T(2,128)(2,1)}), bf16[2,512,1024]{1,0,2:T(2,128)(2,1)}, u32[]{:S(2)}, u32[]{:S(2)}) async-start(bf16[2,512,1024]{1,0,2:T(2,128)(2,1)} %copy.57), calls=%async_computation.4 | async-start | bytes 4194304 | tf_op jit(solution)/shard_map/all_to_all | solution.py:175
  196.1 8.1 copy-start.8
  238.4 8.1 copy-start.8
  278.6 8.2 copy-start.4
  278.6 8.3 copy-start.3
  311.1 3.3 copy-start.2
  346.8 4.3 copy-start.1
  346.9 19.4 %slice-start = ((s8[16777216]{0:T(1024)(128)(4,1)}), s8[4194304]{0:T(1024)(128)(4,1)S(1)}, s32[]{:S(2)}) async-start(s8[16777216]{0:T(1024)(128)(4,1)} %bitcast.276), calls=%async_computation.17 | async-start | bytes 8388608 | tf_op jit(solution)/shard_map/while
  346.9 19.4 %slice-start.1 = ((s8[16777216]{0:T(1024)(128)(4,1)}), s8[4194304]{0:T(1024)(128)(4,1)S(1)}, s32[]{:S(2)}) async-start(s8[16777216]{0:T(1024)(128)(4,1)} %bitcast.276), calls=%async_computation.18 | async-start | bytes 8388608 | tf_op jit(solution)/shard_map/while
  352.2 14.1 slice-start.2
  358.8 7.5 slice-start.3
  367.9 6.2 copy-start.20
  367.9 6.2 copy-start.22
  379.6 8.2 copy-start.4
  379.6 8.3 copy-start.3
  412.1 3.3 copy-start.2
  447.8 4.3 copy-start.1
  447.9 19.4 %slice-start = ((s8[16777216]{0:T(1024)(128)(4,1)}), s8[4194304]{0:T(1024)(128)(4,1)S(1)}, s32[]{:S(2)}) async-start(s8[16777216]{0:T(1024)(128)(4,1)} %bitcast.276), calls=%async_computation.17 | async-start | bytes 8388608 | tf_op jit(solution)/shard_map/while
  447.9 19.4 %slice-start.1 = ((s8[16777216]{0:T(1024)(128)(4,1)}), s8[4194304]{0:T(1024)(128)(4,1)S(1)}, s32[]{:S(2)}) async-start(s8[16777216]{0:T(1024)(128)(4,1)} %bitcast.276), calls=%async_computation.18 | async-start | bytes 8388608 | tf_op jit(solution)/shard_map/while
  453.2 14.1 slice-start.2
  459.8 7.5 slice-start.3
  468.9 6.2 copy-start.20
  468.9 6.2 copy-start.22
  484.6 28.5 %all-to-all-start.5 = ((bf16[2,1024,512]{2,0,1:T(2,128)(2,1)}), bf16[2,1024,512]{2,0,1:T(2,128)(2,1)}, u32[]{:S(2)}, u32[]{:S(2)}) async-start(bf16[2,1024,512]{2,0,1:T(2,128)(2,1)} %copy.59), calls=%async_computation.5 | async-start | bytes 4194304 | tf_op jit(solution)/shard_map/all_to_all | solution.py:227
  505.4 12.5 copy-start.35
  513.1 55.3 %all-to-all-start.6 = ((bf16[2,1024,512]{2,0,1:T(2,128)(2,1)}), bf16[2,1024,512]{2,0,1:T(2,128)(2,1)}, u32[]{:S(2)}, u32[]{:S(2)}) async-start(bf16[2,1024,512]{2,0,1:T(2,128)(2,1)} %copy.63), calls=%async_computation.6 | async-start | bytes 4194304 | tf_op jit(solution)/shard_map/all_to_all | solution.py:230
  568.4 53.5 %all-to-all-start.7 = ((bf16[2,1024,512]{2,0,1:T(2,128)(2,1)}), bf16[2,1024,512]{2,0,1:T(2,128)(2,1)}, u32[]{:S(2)}, u32[]{:S(2)}) async-start(bf16[2,1024,512]{2,0,1:T(2,128)(2,1)} %copy.67), calls=%async_computation.7 | async-start | bytes 4194304 | tf_op jit(solution)/shard_map/all_to_all | solution.py:233
  621.9 55.2 %all-to-all-start.3 = ((bf16[2,1024,512]{2,0,1:T(2,128)(2,1)}), bf16[2,1024,512]{2,0,1:T(2,128)(2,1)}, u32[]{:S(2)}, u32[]{:S(2)}) async-start(bf16[2,1024,512]{2,0,1:T(2,128)(2,1)} %copy.55), calls=%async_computation.3 | async-start | bytes 4194304 | tf_op jit(solution)/shard_map/all_to_all | solution.py:143
  626.8 177.1 %all-reduce.3.cloned.1.call-start = ((), (), s32[]{:S(2)}) async-start(), calls=%async_computation.16 | async-start | bytes 524288 | tf_op jit(solution)/shard_map/psum | solution.py:268
  626.8 5.9 copy-start.10
  626.8 5.9 copy-start.13
  626.8 5.9 copy-start.24
  626.9 5.9 copy-start.25
  626.9 5.9 copy-start.39
  642.3 13.2 copy-start.26
  642.3 13.2 copy-start.27
  642.3 13.2 copy-start.6
  642.3 13.2 copy-start.30
  642.3 13.2 copy-start.32
  642.3 13.2 copy-start.34
  655.5 15.7 copy-start.17
  676.9 270.2 %reduce-scatter.7.cloned.1.call-start = ((), (), s32[]{:S(2)}) async-start(), calls=%async_computation.13 | async-start | bytes 4325376 | tf_op jit(solution)/shard_map/reduce_scatter | solution.py:274
  677.2 5.8 copy-start.18
  687.4 419.0 %reduce-scatter.5.cloned.1.call-start = ((), (), s32[]{:S(2)}) async-start(), calls=%async_computation.12 | async-start | bytes 12976128 | tf_op jit(solution)/shard_map/reduce_scatter | solution.py:273
  700.3 765.3 %reduce-scatter.9.cloned.1.call-start = ((), (), s32[]{:S(2)}) async-start(), calls=%async_computation.14 | async-start | bytes 17301504 | tf_op jit(solution)/shard_map/reduce_scatter | solution.py:275
  716.8 1110.2 %reduce-scatter.11.cloned.1.call-start = ((), (), s32[]{:S(2)}) async-start(), calls=%async_computation.15 | async-start | bytes 17301504 | tf_op jit(solution)/shard_map/reduce_scatter | solution.py:276
  782.0 4.1 copy-start.7
  (13 other events, 22.3 us)
Sparse Core Ops, SparseCore 0:
  677.1 126.2 all-reduce.2
  806.2 140.8 reduce-scatter.6
  953.7 152.6 reduce-scatter.4
  1109.2 356.3 reduce-scatter.8
  1468.5 358.4 reduce-scatter.10
where the time goes:
time: 1840 us
  waiting for transfers between devices  1060 us (58%)
  matrix products  344 us (19%)
  local copies, waits for them, and re-layouts  210 us (11%)
  other arithmetic  124 us (7%)
  blocking collectives  42 us (2%)
  starting transfers between devices  39.3 us (2%)
    reduce_scatter x1, waiting for transfers between devices, body(): lax.psum_scatter(down_grad, ('dp', 'seq'), scatter_dimension=0, tiled=True)  361 us
    reduce_scatter x1, waiting for transfers between devices, body(): lax.psum_scatter(up_grad, ('dp', 'seq'), scatter_dimension=0, tiled=True)  359 us
    reduce_scatter x1, waiting for transfers between devices, body(): lax.psum_scatter(qkv_grad, ('dp', 'seq'), scatter_dimension=0, tiled=True)  159 us
    reduce_scatter x1, waiting for transfers between devices, body(): lax.psum_scatter(out_grad, ('dp', 'seq'), scatter_dimension=0, tiled=True)  143 us
    dot_general x8, matrix products, scores_for(): jnp.einsum('qhd,khd->hqk', query_block, key_rows, preferred_element_type=...  71.4 us
    convert_element_type x4, other arithmetic, attend_back(): scores_grad = (probs_full * (probs_grad - inner_sum)).astype(jnp.bfloat16)  45.3 us
    psum x1, blocking collectives, body(): lax.psum((gain_grad, bias_grad, up_bias_grad, down_bias_grad, family_grad...  42 us
  transfers between devices with their start and end apart: 13, of which 7 were waited for; matrix products, arithmetic and copies ran while one was open for 21% of the time, Pallas kernels for 0%

commit v1 on v0

--- a/solution.py
+++ b/solution.py
@@ -266,8 +266,10 @@
         "rf,rd->fd", orient_hot.astype(jnp.float32), row_sums, precision=lax.Precision.HIGHEST
     )
     gain_sum, bias_sum, up_bias_sum, down_bias_sum, family_sum, orient_sum = lax.psum(
-        (gain_grad, bias_grad, up_bias_grad, down_bias_grad, family_grad, orient_grad),
-        ("dp", "seq"),
+        lax.psum(
+            (gain_grad, bias_grad, up_bias_grad, down_bias_grad, family_grad, orient_grad), "seq"
+        ),
+        "dp",
     )
     qkv_sum, out_sum, up_sum, down_sum = (
         lax.psum_scatter(qkv_grad, ("dp", "seq"), scatter_dimension=0, tiled=True),

time: 1840 us -> 1750 us (0.951)
  waiting for transfers between devices: 1060 us -> 931 us
  blocking collectives: 42 us -> 68.9 us
    reduce_scatter x1, waiting for transfers between devices: 143 us -> 0.01 us  [body(): lax.psum_scatter(out_grad, ('dp', 'seq'), scatter_dimension=0, tiled=True)]
    psum x0 -> x1, blocking collectives: none -> 61.6 us  [body(): lax.psum(lax.psum((gain_grad, bias_grad, up_bias_grad, down_bias_grad, fa...]
    psum x1, blocking collectives: 42 us -> 7.31 us  [body(): lax.psum((gain_grad, bias_grad, up_bias_grad, down_bias_grad, family_grad...]
    psum x1, waiting for transfers between devices: 0.01 us -> 18.8 us  [body(): lax.psum((gain_grad, bias_grad, up_bias_grad, down_bias_grad, family_grad...]
  transfers between devices with their start and end apart: 13 -> 14, of which waited for: 7 -> 7; matrix products, arithmetic and copies ran while one was open for 21% -> 22% of each run, Pallas kernels for 0% -> 0%
where the time goes in v1:
time: 1750 us; the launch traced here: 1740 us
  waiting for transfers between devices  931 us (53%)
  matrix products  346 us (20%)
  local copies, waits for them, and re-layouts  210 us (12%)
  other arithmetic  124 us (7%)
  blocking collectives  68.9 us (4%)
  starting transfers between devices  39.3 us (2%)
    reduce_scatter x1, waiting for transfers between devices, body(): lax.psum_scatter(down_grad, ('dp', 'seq'), scatter_dimension=0, tiled=True)  361 us
    reduce_scatter x1, waiting for transfers between devices, body(): lax.psum_scatter(up_grad, ('dp', 'seq'), scatter_dimension=0, tiled=True)  359 us
    reduce_scatter x1, waiting for transfers between devices, body(): lax.psum_scatter(qkv_grad, ('dp', 'seq'), scatter_dimension=0, tiled=True)  156 us
    dot_general x8, matrix products, scores_for(): jnp.einsum('qhd,khd->hqk', query_block, key_rows, preferred_element_type=...  71.4 us
    psum x1, blocking collectives, body(): lax.psum(lax.psum((gain_grad, bias_grad, up_bias_grad, down_bias_grad, fa...  61.6 us
    convert_element_type x4, other arithmetic, attend_back(): scores_grad = (probs_full * (probs_grad - inner_sum)).astype(jnp.bfloat16)  45.3 us
  transfers between devices with their start and end apart: 14, of which 7 were waited for; matrix products, arithmetic and copies ran while one was open for 22% of the time, Pallas kernels for 0%

profile of v1, /device:TPU:0, one launch (start us, length us, event | category | flops | bytes accessed | tf_op | source)
XLA Modules:
  0.0 1738.3 jit_solution(17315400432831193795)
XLA Ops:
  15.9 7.0 fusion.30
  22.9 7.9 fusion.89
  33.9 7.5 fusion.48
  41.5 12.5 fusion.37
  54.0 6.2 copy.51
  65.0 6.2 copy.53
  71.2 20.2 %all-to-all-done.1 = bf16[2,512,1024]{1,0,2:T(2,128)(2,1)} async-done(((bf16[2,512,1024]{1,0,2:T(2,128)(2,1)}), bf16[2,512,1024]{1,0,2:T(2,128)(2,1)}, u32[]{:S(2)}, u32[]{:S(2)}) %all-to-all-start.1) | async-done | bytes 2097184 | tf_op jit(solution)/shard_map/all_to_all | solution.py:104
  100.1 6.2 copy.49
  106.3 14.7 all-to-all-done.2
  131.2 6.2 copy.57
  177.6 84.7 %while.26 = (s32[]{:T(128)}, bf16[2,1024,512]{1,2,0:T(8,128)(2,1)}, f32[2,8,1024]{2,1,0:T(8,128)S(1)}, bf16[2,1024,512]{1,2,0:T(8,128)(2,1)}, bf16[2,1024,512]{1...) while((s32[]{:T(128)}, bf16[2,1024,512]{1,2,0:T(8,128)(2,1)}, ...), condition=%wide.region_7.8_spmd, body=%wide.region_2.7_spmd.sunk | while | flops 2251817472 | bytes 124064400 | solution.py:140
  189.5 7.4 fusion.195
  196.9 8.1 fusion.196
  205.1 5.6 fusion.200
  210.7 8.2 fusion.197
  231.9 7.4 fusion.195
  239.3 8.1 fusion.196
  247.4 5.6 fusion.200
  253.0 8.2 fusion.197
  276.7 202.6 %while.27 = (s32[]{:T(128)}, bf16[2,1024,512]{1,2,0:T(8,128)(2,1)}, bf16[2,1024,512]{1,2,0:T(8,128)(2,1)}, bf16[2,1024,512]{1,2,0:T(8,128)(2,1)}, bf16[2,1024,51...) while((s32[]{:T(128)}, bf16[2,1024,512]{1,2,0:T(8,128)(2,1)}, ...), condition=%wide.region_11.12_spmd, body=%wide.region_8.11_spmd.sunk | while | flops 5451014656 | bytes 458462208 | solution.py:223
  279.5 8.1 fusion.226
  288.0 12.6 multiply_reduce_fusion.9
  300.6 11.3 multiply_convert_fusion.10
  315.2 8.1 fusion.223
  323.7 12.6 multiply_reduce_fusion.8
  336.4 11.3 multiply_convert_fusion.9
  353.0 6.6 fusion.227
  359.6 7.5 fusion.228
  368.8 6.2 fusion.225
  380.5 8.1 fusion.226
  389.0 12.6 multiply_reduce_fusion.9
  401.6 11.3 multiply_convert_fusion.10
  416.2 8.1 fusion.223
  424.7 12.6 multiply_reduce_fusion.8
  437.4 11.3 multiply_convert_fusion.9
  454.1 6.6 fusion.227
  460.7 7.5 fusion.228
  469.8 6.2 fusion.225
  479.3 6.2 copy.59
  490.3 16.0 fusion.98
  506.3 6.2 copy.63
  518.8 26.5 %convert_reduce_fusion = (f32[4096]{0:T(1024)}, bf16[1024,4096]{1,0:T(8,128)(2,1)}) fusion(f32[1024,4096]{1,0:T(8,128)} %fusion.98, f32[4096]{0:T(1024)S(1)} %copy-done.33, bf16[1024,1024]{1,0:T(8,128)(2,1)} %bitcast.316, bf16[4096,1024]{1,0:T(8,128)(2,1)} %param.27), kind=kOutput, calls=%fused_computation.70 | convolution fusion | flops 8686399488 | bytes 35684352 | tf_op jit(solution)/shard_map/nd,fd->nf/dot_general | solution.py:164
  545.3 6.2 copy.67
  551.5 6.3 copy.55
  557.8 5.8 copy.78
  563.6 5.8 copy.60
  574.2 5.8 copy.77
  580.0 5.7 copy.64
  585.7 6.8 reshape.472
  592.6 6.7 reshape.474
  633.7 9.5 fusion.33
  643.3 13.1 fusion.46
  656.5 15.7 multiply_reduce_fusion.2
  683.8 18.8 %all-reduce.5.cloned.1.call-done = f32[64,1024]{1,0:T(8,128)} async-done(((f32[64,1024]{1,0:T(8,128)}), f32[64,1024]{1,0:T(8,128)}) %all-reduce.5.cloned.1.call-update) | async-done | bytes 262160 | tf_op jit(solution)/shard_map/psum | solution.py:269
  702.7 6.6 fusion.99
  709.3 12.8 fusion.45
  722.5 16.2 fusion.100
  738.8 20.2 %fusion.85 = f32[4096,1024]{1,0:T(8,128)} fusion(bf16[1024,1024]{1,0:T(8,128)(2,1)} %bitcast.318, f32[1024,4096]{1,0:T(8,128)} %fusion.98, f32[4096]{0:T(1024)S(1)} %copy-done.33), kind=kOutput, calls=%fused_computation.174 | convolution fusion | flops 8631877632 | bytes 35667968 | tf_op jit(solution)/shard_map/nf,nd->fd/dot_general | solution.py:162
  761.9 7.3 all-reduce.1
  769.3 61.6 %all-reduce = (f32[1024]{0:T(1024)}, f32[1024]{0:T(1024)}, f32[4096]{0:T(1024)}, f32[1024]{0:T(1024)}, f32[2,1024]{1,0:T(2,128)}) all-reduce(f32[1024]{0:T(1024)S(1)} %get-tuple-element.138, f32[1024]{0:T(1024)S(1)} %get-tuple-element.139, f32[4096]{0:T(1024)S(1)} %get-tuple-element.140, ...), channel_id=1, replica_groups=mesh['dp'=16,'seq'=2] {'dp'}, use_global_device_ids=true, to_apply=%region_16.17 | all-reduce | flops 9216 | bytes 73728 | tf_op jit(solution)/shard_map/psum | solution.py:268
  834.9 17.8 %fusion.43 = bf16[1024,1024]{1,0:T(8,128)(2,1)} fusion(f32[1024,1024]{1,0:T(8,128)S(1)} %fusion.97, f32[2,512,1024]{2,1,0:T(8,128)S(1)} %copy-done.7, f32[1024]{0:T(1024)S(1)} %convert_element_type.217, bf16[4096,1024]{1,0:T(8,128)(2,1)} %param.27, f32[1024,4096]{1,0:T(8,128)} %fusion.98, f32[4096]{0:T(1024)S(1)} %copy-done.33), kind=kOutput, calls=%fused_computation.97 | convolution fusion | flops 8636071936 | bytes 35672064 | tf_op jit(solution)/shard_map/dot_general | solution.py:152
  852.7 155.8 %reduce-scatter.5.cloned.1.call-done = f32[32,3072]{1,0:T(8,128)} async-done(((f32[1024,3072]{1,0:T(8,128)}), f32[32,3072]{1,0:T(8,128)}) %reduce-scatter.5.cloned.1.call-update) | async-done | bytes 393232 | tf_op jit(solution)/shard_map/reduce_scatter | solution.py:275
  1008.5 358.8 %reduce-scatter.9.cloned.1.call-done = f32[32,4096]{1,0:T(8,128)} async-done(((f32[1024,4096]{1,0:T(8,128)}), f32[32,4096]{1,0:T(8,128)}) %reduce-scatter.9.cloned.1.call-update) | async-done | bytes 524304 | tf_op jit(solution)/shard_map/reduce_scatter | solution.py:277
  1367.3 361.4 %reduce-scatter.11.cloned.1.call-done = f32[128,1024]{1,0:T(8,128)} async-done(((f32[4096,1024]{1,0:T(8,128)}), f32[128,1024]{1,0:T(8,128)}) %reduce-scatter.11.cloned.1.call-update) | async-done | bytes 524304 | tf_op jit(solution)/shard_map/reduce_scatter | solution.py:278
  (258 shorter events, 218.3 us)
Async XLA Ops:
  8.0 117.9 %copy-start = (bf16[1024,1024]{1,0:T(8,128)(2,1)S(1)}, bf16[1024,1024]{1,0:T(8,128)(2,1)}, u32[]{:S(2)}) copy-start(bf16[1024,1024]{1,0:T(8,128)(2,1)} %param.24) | copy-start | bytes 6291460
  8.0 7.0 copy-start.18
  10.9 5.0 copy-start.40
  10.9 5.0 copy-start.41
  10.9 5.0 copy-start.43
  15.9 122.1 %copy-start.27 = (f32[1024]{0:T(1024)}, f32[1024]{0:T(1024)S(1)}, u32[]{:S(2)}) copy-start(f32[1024]{0:T(1024)S(1)} %convert_element_type.207) | copy-start | bytes 12292
  22.9 9.6 copy-start.5
  33.9 20.2 %copy-start.36 = (pred[1024]{0:T(1024)(128)(4,1)}, pred[1024]{0:T(1024)(128)(4,1)S(1)}, u32[]{:S(2)}) copy-start(pred[1024]{0:T(1024)(128)(4,1)S(1)} %fusion.61) | copy-start | bytes 3076
  33.9 7.6 copy-start.16
  41.5 12.6 copy-start.9
  41.5 12.6 copy-start.11
  60.2 31.2 %all-to-all-start.1 = ((bf16[2,512,1024]{1,0,2:T(2,128)(2,1)}), bf16[2,512,1024]{1,0,2:T(2,128)(2,1)}, u32[]{:S(2)}, u32[]{:S(2)}) async-start(bf16[2,512,1024]{1,0,2:T(2,128)(2,1)} %copy.51), calls=%async_computation.1 | async-start | bytes 4194304 | tf_op jit(solution)/shard_map/all_to_all | solution.py:104
  91.4 29.5 %all-to-all-start.2 = ((bf16[2,512,1024]{1,0,2:T(2,128)(2,1)}), bf16[2,512,1024]{1,0,2:T(2,128)(2,1)}, u32[]{:S(2)}, u32[]{:S(2)}) async-start(bf16[2,512,1024]{1,0,2:T(2,128)(2,1)} %copy.53), calls=%async_computation.2 | async-start | bytes 4194304 | tf_op jit(solution)/shard_map/all_to_all | solution.py:105
  120.9 40.4 %all-to-all-start = ((bf16[2,512,1024]{1,0,2:T(2,128)(2,1)}), bf16[2,512,1024]{1,0,2:T(2,128)(2,1)}, u32[]{:S(2)}, u32[]{:S(2)}) async-start(bf16[2,512,1024]{1,0,2:T(2,128)(2,1)} %copy.49), calls=%async_computation | async-start | bytes 4194304 | tf_op jit(solution)/shard_map/all_to_all | solution.py:106
  131.2 6.2 copy-start.35
  137.4 4.9 copy-start.29
  137.4 4.9 copy-start.31
  161.3 101.0 %all-to-all-start.4 = ((bf16[2,512,1024]{1,0,2:T(2,128)(2,1)}), bf16[2,512,1024]{1,0,2:T(2,128)(2,1)}, u32[]{:S(2)}, u32[]{:S(2)}) async-start(bf16[2,512,1024]{1,0,2:T(2,128)(2,1)} %copy.57), calls=%async_computation.4 | async-start | bytes 4194304 | tf_op jit(solution)/shard_map/all_to_all | solution.py:175
  196.9 8.1 copy-start.8
  239.3 8.1 copy-start.8
  279.5 8.2 copy-start.4
  279.5 8.3 copy-start.3
  312.0 3.3 copy-start.2
  347.7 4.3 copy-start.1
  347.7 19.4 %slice-start = ((s8[16777216]{0:T(1024)(128)(4,1)}), s8[4194304]{0:T(1024)(128)(4,1)S(1)}, s32[]{:S(2)}) async-start(s8[16777216]{0:T(1024)(128)(4,1)} %bitcast.276), calls=%async_computation.18 | async-start | bytes 8388608 | tf_op jit(solution)/shard_map/while
  347.7 19.4 %slice-start.1 = ((s8[16777216]{0:T(1024)(128)(4,1)}), s8[4194304]{0:T(1024)(128)(4,1)S(1)}, s32[]{:S(2)}) async-start(s8[16777216]{0:T(1024)(128)(4,1)} %bitcast.276), calls=%async_computation.19 | async-start | bytes 8388608 | tf_op jit(solution)/shard_map/while
  353.0 14.1 slice-start.2
  359.6 7.5 slice-start.3
  368.8 6.2 copy-start.19
  368.8 6.2 copy-start.21
  380.5 8.2 copy-start.4
  380.5 8.3 copy-start.3
  413.0 3.3 copy-start.2
  448.7 4.3 copy-start.1
  448.7 19.4 %slice-start = ((s8[16777216]{0:T(1024)(128)(4,1)}), s8[4194304]{0:T(1024)(128)(4,1)S(1)}, s32[]{:S(2)}) async-start(s8[16777216]{0:T(1024)(128)(4,1)} %bitcast.276), calls=%async_computation.18 | async-start | bytes 8388608 | tf_op jit(solution)/shard_map/while
  448.7 19.4 %slice-start.1 = ((s8[16777216]{0:T(1024)(128)(4,1)}), s8[4194304]{0:T(1024)(128)(4,1)S(1)}, s32[]{:S(2)}) async-start(s8[16777216]{0:T(1024)(128)(4,1)} %bitcast.276), calls=%async_computation.19 | async-start | bytes 8388608 | tf_op jit(solution)/shard_map/while
  454.1 14.1 slice-start.2
  460.6 7.5 slice-start.3
  469.8 6.2 copy-start.19
  469.8 6.2 copy-start.21
  485.5 28.6 %all-to-all-start.5 = ((bf16[2,1024,512]{2,0,1:T(2,128)(2,1)}), bf16[2,1024,512]{2,0,1:T(2,128)(2,1)}, u32[]{:S(2)}, u32[]{:S(2)}) async-start(bf16[2,1024,512]{2,0,1:T(2,128)(2,1)} %copy.59), calls=%async_computation.5 | async-start | bytes 4194304 | tf_op jit(solution)/shard_map/all_to_all | solution.py:227
  506.3 12.5 copy-start.33
  514.0 55.3 %all-to-all-start.6 = ((bf16[2,1024,512]{2,0,1:T(2,128)(2,1)}), bf16[2,1024,512]{2,0,1:T(2,128)(2,1)}, u32[]{:S(2)}, u32[]{:S(2)}) async-start(bf16[2,1024,512]{2,0,1:T(2,128)(2,1)} %copy.63), calls=%async_computation.6 | async-start | bytes 4194304 | tf_op jit(solution)/shard_map/all_to_all | solution.py:230
  569.3 53.6 %all-to-all-start.7 = ((bf16[2,1024,512]{2,0,1:T(2,128)(2,1)}), bf16[2,1024,512]{2,0,1:T(2,128)(2,1)}, u32[]{:S(2)}, u32[]{:S(2)}) async-start(bf16[2,1024,512]{2,0,1:T(2,128)(2,1)} %copy.67), calls=%async_computation.7 | async-start | bytes 4194304 | tf_op jit(solution)/shard_map/all_to_all | solution.py:233
  622.9 55.2 %all-to-all-start.3 = ((bf16[2,1024,512]{2,0,1:T(2,128)(2,1)}), bf16[2,1024,512]{2,0,1:T(2,128)(2,1)}, u32[]{:S(2)}, u32[]{:S(2)}) async-start(bf16[2,1024,512]{2,0,1:T(2,128)(2,1)} %copy.55), calls=%async_computation.3 | async-start | bytes 4194304 | tf_op jit(solution)/shard_map/all_to_all | solution.py:143
  627.7 74.9 %all-reduce.5.cloned.1.call-start = ((), (), s32[]{:S(2)}) async-start(), calls=%async_computation.16 | async-start | bytes 524288 | tf_op jit(solution)/shard_map/psum | solution.py:269
  627.8 5.9 copy-start.10
  627.8 5.9 copy-start.13
  627.8 5.9 copy-start.23
  627.8 5.9 copy-start.24
  627.8 5.9 copy-start.37
  643.3 13.2 copy-start.25
  643.3 13.2 copy-start.26
  643.3 13.2 copy-start.6
  643.3 13.2 copy-start.28
  643.3 13.2 copy-start.30
  643.3 13.2 copy-start.32
  656.5 15.7 copy-start.17
  677.9 174.8 %all-reduce.7.cloned.1.call-start = ((), (), s32[]{:S(2)}) async-start(), calls=%async_computation.17 | async-start | bytes 524288 | tf_op jit(solution)/shard_map/psum | solution.py:268
  702.6 150.1 %reduce-scatter.7.cloned.1.call-start = ((), (), s32[]{:S(2)}) async-start(), calls=%async_computation.13 | async-start | bytes 4325376 | tf_op jit(solution)/shard_map/reduce_scatter | solution.py:276
  709.3 299.2 %reduce-scatter.5.cloned.1.call-start = ((), (), s32[]{:S(2)}) async-start(), calls=%async_computation.12 | async-start | bytes 12976128 | tf_op jit(solution)/shard_map/reduce_scatter | solution.py:275
  722.2 645.1 %reduce-scatter.9.cloned.1.call-start = ((), (), s32[]{:S(2)}) async-start(), calls=%async_computation.14 | async-start | bytes 17301504 | tf_op jit(solution)/shard_map/reduce_scatter | solution.py:277
  738.7 990.0 %reduce-scatter.11.cloned.1.call-start = ((), (), s32[]{:S(2)}) async-start(), calls=%async_computation.15 | async-start | bytes 17301504 | tf_op jit(solution)/shard_map/reduce_scatter | solution.py:278
  830.9 4.1 copy-start.7
  (12 other events, 21.0 us)
Sparse Core Ops, SparseCore 0:
  678.0 24.5 all-reduce.4
  706.0 89.3 all-reduce.6
Sparse Core Ops, SparseCore 1:
  709.4 141.5 reduce-scatter.6
  857.4 151.1 reduce-scatter.4
  1011.4 355.9 reduce-scatter.8
  1370.3 358.3 reduce-scatter.10
